TPU v7x, 256 devices: a whole 4x4x8 slice. The times are simulated.
256 devices in a mesh: nodes: 64 (over x, z, core), feat: 4 (over y).
Axes of the slice: x: 4, y: 4, z: 8, core: 2. Of those that a mesh axis runs over, the one named last changes fastest.
Arguments:
- node_feats: bfloat16 [32768, 512], P('nodes', 'feat'), may hold values from -6 to 6
- weight_one: bfloat16 [512, 512], replicated, may hold values from -0.25 to 0.25
- weight_two: bfloat16 [512, 512], replicated, may hold values from -0.25 to 0.25
- adj_tiles: bfloat16 [256, 24, 128, 128], P('nodes'), may hold values from -0.109375 to 0.109375
- tile_owner: int32 [6144, 1], P('nodes'), may hold values from 0 to 63; in each aligned block of 96 rows (0 to 95, 96 to 191, ...) at most 2 rows name the same one
- tile_local: int32 [6144, 1], P('nodes'), may hold values from 0 to 3
- cotangent: bfloat16 [32768, 512], P('nodes', 'feat'), may hold values from -6 to 6
Outputs:
- layer_output: bfloat16 [32768, 512], P('nodes', 'feat')
- grad_one: float32 [512, 512], P('feat')
- grad_two: float32 [512, 512], P('feat')
Inputs may be any that keep to these rules, and one draw needn't show every extreme that they name: `tile_owner`: among the 96 tiles of one index of nodes, each owner index is named by at most 2 tiles, and exactly 2 for some owner.
All inputs are finite; a program needn't handle non-finite values.
Results may differ from a plain program's by a relative error of at most 0.0065.
Values may be sent and summed in bfloat16 or wider, within the bound.
No kernel may reach another device: no remote copies, remote signals or barrier semaphores. Data moves between devices by JAX's collectives and lax.ppermute only.
A program may use at most 128 MiB of HBM per device.

v0:
```python
import math
import jax
import jax.numpy as jnp
from jax import lax
from jax.sharding import PartitionSpec as P


def plan_slots(tile_owner, tile_local, node_count, capacity):
    owners = tile_owner[:, 0]
    local_ids = tile_local[:, 0]
    hits = (owners[:, None] == jnp.arange(node_count, dtype=jnp.int32)[None, :]).astype(jnp.int32)
    earlier = jnp.cumsum(hits, axis=0) - hits
    ranks = jnp.sum(earlier * hits, axis=1)
    slots = owners * capacity + ranks
    table = jnp.full((node_count * capacity,), -1, jnp.int32).at[slots].set(local_ids)
    source = (
        jnp.zeros((node_count * capacity,), jnp.int32)
        .at[slots]
        .set(jnp.arange(owners.shape[0], dtype=jnp.int32))
    )
    return (slots, table.reshape(node_count, capacity), source)


def body(node_feats, weight_one, weight_two, adj_tiles, tile_owner, tile_local, cotangent):
    node_count = lax.axis_size("nodes")
    blocks_dev = adj_tiles.shape[0]
    per_block = adj_tiles.shape[1]
    block_size = adj_tiles.shape[2]
    tile_total = blocks_dev * per_block
    capacity = max(2, (4 * tile_total + 3 * node_count - 1) // (3 * node_count))
    width = node_feats.shape[1]
    feat_index = lax.axis_index("feat")
    slots, requests, source = plan_slots(tile_owner, tile_local, node_count, capacity)
    asked = lax.all_to_all(requests, "nodes", split_axis=0, concat_axis=0, tiled=True)
    columns = tile_owner[:, 0] * blocks_dev + tile_local[:, 0]

    def spread(features):
        whole = lax.all_gather(features, "nodes", axis=0, tiled=True)
        picked = whole.reshape(-1, block_size, width)[columns]
        picked = picked.reshape(blocks_dev, per_block, block_size, width)
        summed = jnp.einsum("bkij,bkjf->bif", adj_tiles, picked, preferred_element_type=jnp.float32)
        return summed.reshape(-1, width).astype(jnp.bfloat16)

    def mixing(propagated, weights):
        weight_rows = lax.dynamic_slice_in_dim(weights, feat_index * width, width, 0)
        partial_z = jnp.dot(propagated, weight_rows, preferred_element_type=jnp.float32)
        result = lax.psum_scatter(partial_z, "feat", scatter_dimension=1, tiled=True)
        return result

    prop_one = spread(node_feats)
    z_one = mixing(prop_one, weight_one)
    hidden = (z_one * jax.nn.sigmoid(z_one)).astype(jnp.bfloat16)
    prop_two = spread(hidden)
    layer_output = mixing(prop_two, weight_two).astype(jnp.bfloat16)
    factor = 1.0 / math.sqrt(node_feats.shape[0] * node_count)
    contract_rows = (((0,), (0,)), ((), ()))
    cot_full = lax.all_gather(cotangent, "feat", axis=1, tiled=True)
    grad_two = (
        lax.dot_general(prop_two, cot_full, contract_rows, preferred_element_type=jnp.float32)
        * factor
    )
    weight_slice = lax.dynamic_slice_in_dim(weight_two, feat_index * width, width, 0)
    grad_prop = lax.dot_general(
        cot_full, weight_slice, (((1,), (1,)), ((), ())), preferred_element_type=jnp.float32
    ).astype(jnp.bfloat16)
    grad_blocks = grad_prop.reshape(blocks_dev, block_size, width)
    terms = jnp.einsum("bkji,bjf->bkif", adj_tiles, grad_blocks, preferred_element_type=jnp.float32)
    packed = terms.reshape(tile_total, block_size, width)[source].reshape(
        node_count, capacity, block_size, width
    )
    returned = lax.all_to_all(packed, "nodes", split_axis=0, concat_axis=0, tiled=True)
    slot_terms = returned.reshape(-1, block_size, width)
    selector = (
        asked.reshape(-1)[:, None] == jnp.arange(blocks_dev, dtype=jnp.int32)[None, :]
    ).astype(jnp.float32)
    grad_hidden = jnp.einsum(
        "sl,sif->lif", selector, slot_terms, precision=lax.Precision.HIGHEST
    ).reshape(-1, width)
    sigma = jax.nn.sigmoid(z_one)
    grad_z = (grad_hidden * sigma * (1.0 + z_one * (1.0 - sigma))).astype(jnp.bfloat16)
    grad_full = lax.all_gather(grad_z, "feat", axis=1, tiled=True)
    grad_one = (
        lax.dot_general(prop_one, grad_full, contract_rows, preferred_element_type=jnp.float32)
        * factor
    )
    grad_one, grad_two = lax.psum((grad_one, grad_two), "nodes")
    return (layer_output, grad_one, grad_two)


def solution(mesh):
    placed = (
        P("nodes", "feat"),
        P(),
        P(),
        P("nodes", None, None, None),
        P("nodes", None),
        P("nodes", None),
        P("nodes", "feat"),
    )
    return jax.shard_map(
        body,
        mesh=mesh,
        in_specs=placed,
        out_specs=(P("nodes", "feat"), P("feat", None), P("feat", None)),
        check_vma=False,
    )
```

profile of v0, /device:TPU:2, one launch (start us, length us, event | category | flops | bytes accessed | tf_op | source)
XLA Modules:
  0.0 596.0 jit_solution(3835139693002042372)
XLA Ops:
  12.3 12.0 %all-to-all-start = ((s32[64,1,2]{2,1,0:T(1,128)}), s32[64,1,2]{2,1,0:T(1,128)S(1)}, u32[]{:S(2)}, u32[]{:S(2)}) async-start(s32[64,1,2]{2,1,0:T(1,128)} %bitcast.18), calls=%async_computation.2 | async-start | bytes 65536 | tf_op jit(solution)/shard_map/all_to_all | solution.py:34
  24.3 14.3 %all_gather.14 = bf16[512,512]{1,0:T(8,128)(2,1)S(1)} all-gather(bf16[512,128]{1,0:T(8,128)(2,1)} %param.13), channel_id=1, replica_groups=mesh['nodes'=64,'feat'=4] {'feat'}, dimensions={1}, use_global_device_ids=true | all-gather | bytes 655360 | tf_op jit(solution)/shard_map/all_gather | solution.py:57
  41.6 3.5 fusion.5
  45.1 6.6 %copy.27 = f32[96,128,128]{2,1,0:T(8,128)} copy(f32[96,128,128]{1,2,0:T(8,128)} %bitcast.65) | data formatting | bytes 12582912 | tf_op jit(solution)/shard_map/reshape | solution.py:68
  51.8 7.1 %gather_fusion.2 = f32[128,128,128]{2,1,0:T(8,128)} fusion(f32[96,128,128]{2,1,0:T(8,128)} %copy.27, s32[1024]{0:T(1024)S(1)} %pad_clamp_fusion), kind=kCustom, calls=%fused_computation.2 | custom fusion | bytes 16777728 | tf_op jit(solution)/shard_map/gather | solution.py:68
  58.8 15.3 %copy.28 = f32[64,2,128,128]{3,1,2,0:T(2,128)} copy(f32[64,2,128,128]{3,2,1,0:T(8,128)} %bitcast.63) | data formatting | bytes 16777216 | tf_op jit(solution)/shard_map/reshape | solution.py:68
  74.1 10.7 %all-to-all-start.1 = ((f32[64,2,128,128]{3,1,2,0:T(2,128)}), f32[64,2,128,128]{3,1,2,0:T(2,128)}, u32[]{:S(2)}, u32[]{:S(2)}) async-start(f32[64,2,128,128]{3,1,2,0:T(2,128)} %copy.28), calls=%async_computation.3 | async-start | bytes 16777216 | tf_op jit(solution)/shard_map/all_to_all | solution.py:71
  84.9 22.9 %all-gather.3.cloned.1.call-done = bf16[32768,128]{1,0:T(8,128)(2,1)} async-done(((bf16[512,128]{1,0:T(8,128)(2,1)}), bf16[32768,128]{1,0:T(8,128)(2,1)}) %all-gather.3.cloned.1.call-update) | async-done | bytes 8388624 | tf_op jit(solution)/shard_map/all_gather | solution.py:38
  107.8 6.2 %gather_fusion = bf16[96,128,128]{2,1,0:T(8,128)(2,1)} fusion(bf16[256,128,128]{2,1,0:T(8,128)(2,1)} %bitcast.72, s32[1024]{0:T(1024)S(1)} %pad_clamp_fusion.1), kind=kCustom, calls=%fused_computation | custom fusion | bytes 6291840 | tf_op jit(solution)/shard_map/gather | solution.py:39
  114.0 2.9 fusion
  116.8 2.1 fusion.7
  120.6 151.2 %all-to-all-done.1 = f32[64,2,128,128]{3,1,2,0:T(2,128)} async-done(((f32[64,2,128,128]{3,1,2,0:T(2,128)}), f32[64,2,128,128]{3,1,2,0:T(2,128)}, u32[]{:S(2)}, u32[]{:S(2)}) %all-to-all-start.1) | async-done | bytes 8388640 | tf_op jit(solution)/shard_map/all_to_all | solution.py:71
  271.8 6.1 %copy.29 = f32[64,2,128,128]{3,1,0,2:T(2,128)S(1)} copy(f32[64,2,128,128]{3,1,2,0:T(2,128)} %all-to-all-done.1) | data formatting | bytes 16777216 | tf_op jit(solution)/shard_map/all_to_all | solution.py:71
  277.9 2.8 fusion.14
  280.8 1.8 fusion.4
  282.6 80.6 %all-gather.5.cloned.1.call-done = bf16[32768,128]{1,0:T(8,128)(2,1)} async-done(((bf16[512,128]{1,0:T(8,128)(2,1)}), bf16[32768,128]{1,0:T(8,128)(2,1)}) %all-gather.5.cloned.1.call-update) | async-done | bytes 8388624 | tf_op jit(solution)/shard_map/all_gather | solution.py:38
  363.3 6.2 %gather_fusion.1 = bf16[96,128,128]{2,1,0:T(8,128)(2,1)} fusion(bf16[256,128,128]{2,1,0:T(8,128)(2,1)} %bitcast.73, s32[1024]{0:T(1024)S(1)} %pad_clamp_fusion.1), kind=kCustom, calls=%fused_computation.1 | custom fusion | bytes 6291840 | tf_op jit(solution)/shard_map/gather | solution.py:39
  369.4 2.9 fusion.1
  372.3 2.2 fusion.10
  374.6 16.3 %all_gather.15 = bf16[512,512]{1,0:T(8,128)(2,1)S(1)} all-gather(bf16[512,128]{1,0:T(8,128)(2,1)S(1)} %copy-done.2), channel_id=1, replica_groups=mesh['nodes'=64,'feat'=4] {'feat'}, dimensions={1}, use_global_device_ids=true | all-gather | bytes 655360 | tf_op jit(solution)/shard_map/all_gather | solution.py:81
  391.8 2.0 convolution_multiply_fusion
  393.8 6.3 %reduce-scatter.5.cloned.1.call-done = f32[512,128]{1,0:T(8,128)} async-done(((f32[512,512]{1,0:T(8,128)}), f32[512,128]{1,0:T(8,128)}) %reduce-scatter.5.cloned.1.call-update) | async-done | bytes 262160 | tf_op jit(solution)/shard_map/reduce_scatter | solution.py:47
  401.8 184.4 %all-reduce.3.cloned.1.call-done = (f32[128,512]{1,0:T(8,128)}, f32[128,512]{1,0:T(8,128)}) async-done(((f32[128,512]{1,0:T(8,128)}, f32[128,512]{1,0:T(8,128)}), (f32[128,512]{1,0:T(8,128)}, f32[128,512]{1,0:T(8,128)})) %all-reduce.3.cloned.1.call-update) | async-done | bytes 524304 | tf_op jit(solution)/shard_map/psum | solution.py:86
  586.2 1.7 copy.40
  (38 shorter events, 14.1 us)
Async XLA Ops:
  7.2 34.4 %copy-start = (bf16[4,24,128,128]{3,2,1,0:T(8,128)(2,1)S(1)}, bf16[4,24,128,128]{3,2,1,0:T(8,128)(2,1)}, u32[]{:S(2)}) copy-start(bf16[4,24,128,128]{3,2,1,0:T(8,128)(2,1)} %param.10) | copy-start | bytes 9437188
  7.2 100.6 %all-gather.3.cloned.1.call-start = ((), (), s32[]{:S(2)}) async-start(), calls=%async_computation.4 | async-start | bytes 8519680 | tf_op jit(solution)/shard_map/all_gather | solution.py:38
  12.3 61.9 %all-to-all-start = ((s32[64,1,2]{2,1,0:T(1,128)}), s32[64,1,2]{2,1,0:T(1,128)S(1)}, u32[]{:S(2)}, u32[]{:S(2)}) async-start(s32[64,1,2]{2,1,0:T(1,128)} %bitcast.18), calls=%async_computation.2 | async-start | bytes 65536 | tf_op jit(solution)/shard_map/all_to_all | solution.py:34
  38.6 0.8 copy-start.1
  74.1 197.6 %all-to-all-start.1 = ((f32[64,2,128,128]{3,1,2,0:T(2,128)}), f32[64,2,128,128]{3,1,2,0:T(2,128)}, u32[]{:S(2)}, u32[]{:S(2)}) async-start(f32[64,2,128,128]{3,1,2,0:T(2,128)} %copy.28), calls=%async_computation.3 | async-start | bytes 16777216 | tf_op jit(solution)/shard_map/all_to_all | solution.py:71
  84.8 195.9 %reduce-scatter.3.cloned.1.call-start = ((), (), s32[]{:S(2)}) async-start(), calls=%async_computation.5 | async-start | bytes 1310720 | tf_op jit(solution)/shard_map/reduce_scatter | solution.py:47
  119.0 244.3 %all-gather.5.cloned.1.call-start = ((), (), s32[]{:S(2)}) async-start(), calls=%async_computation.6 | async-start | bytes 8519680 | tf_op jit(solution)/shard_map/all_gather | solution.py:38
  282.6 117.5 %reduce-scatter.5.cloned.1.call-start = ((), (), s32[]{:S(2)}) async-start(), calls=%async_computation.7 | async-start | bytes 1310720 | tf_op jit(solution)/shard_map/reduce_scatter | solution.py:47
  369.4 5.1 copy-start.2
  374.5 211.7 %all-reduce.3.cloned.1.call-start = ((), (), s32[]{:S(2)}) async-start(), calls=%async_computation.8 | async-start | bytes 1048576 | tf_op jit(solution)/shard_map/psum | solution.py:86
Sparse Core Ops, SparseCore 0:
  10.8 96.9 all-gather.2
  119.1 28.1 reduce-scatter.2
  282.7 80.4 all-gather.4
  374.6 25.4 reduce-scatter.4
  404.1 182.0 all-reduce.2
where the time goes:
time: 597 us; the launch traced here: 596 us
  waiting for transfers between devices  446 us (75%)
  local copies, waits for them, and re-layouts  54.9 us (9%)
  blocking collectives  30.6 us (5%)
  starting transfers between devices  23.1 us (4%)
  matrix products  20.6 us (3%)
  between operations  13.9 us (2%)
  other arithmetic  6.74 us (1%)
    psum x1, waiting for transfers between devices, body(): grad_one, grad_two = lax.psum((grad_one, grad_two), 'nodes')  184 us
    all_to_all x1, waiting for transfers between devices, body(): lax.all_to_all(packed, 'nodes', split_axis=0, concat_axis=0, tiled=True)  151 us
    all_gather x2, waiting for transfers between devices, spread(): whole = lax.all_gather(features, 'nodes', axis=0, tiled=True)  104 us
    reshape x2, local copies, waits for them, and re-layouts, body(): terms.reshape(tile_total, block_size, width)[source]  22 us
    all_gather x1, blocking collectives, body(): grad_full = lax.all_gather(grad_z, 'feat', axis=1, tiled=True)  16.3 us
    all_gather x1, blocking collectives, body(): cot_full = lax.all_gather(cotangent, 'feat', axis=1, tiled=True)  14.3 us
    gather x2, local copies, waits for them, and re-layouts, spread(): picked = whole.reshape(-1, block_size, width)[columns]  12.3 us
    all_to_all x1, starting transfers between devices, body(): lax.all_to_all(requests, 'nodes', split_axis=0, concat_axis=0, tiled=True)  12 us
  transfers between devices with their start and end apart: 7, of which 5 were waited for; matrix products, arithmetic and copies ran while one was open for 11% of the time, Pallas kernels for 0%

commit v1 on v0

--- a/solution.py
+++ b/solution.py
@@ -35,7 +35,9 @@
     columns = tile_owner[:, 0] * blocks_dev + tile_local[:, 0]
 
     def spread(features):
-        whole = lax.all_gather(features, "nodes", axis=0, tiled=True)
+        whole = jnp.concatenate(
+            lax.all_to_all(jnp.stack([features] * lax.axis_size("nodes")), "nodes", 0, 0), axis=0
+        )
         picked = whole.reshape(-1, block_size, width)[columns]
         picked = picked.reshape(blocks_dev, per_block, block_size, width)
         summed = jnp.einsum("bkij,bkjf->bif", adj_tiles, picked, preferred_element_type=jnp.float32)

time: 597 us -> 859 us (1.44)
  blocking collectives: 30.6 us -> 242 us
  waiting for transfers between devices: 446 us -> 497 us
  starting transfers between devices: 23.1 us -> 14.5 us
    all_to_all x0 -> x2, blocking collectives: none -> 212 us  [the longest x1 191 us: spread(): lax.all_to_all(jnp.stack([features] * lax.axis_size('nodes')), 'nodes', 0...]
    all_to_all x1, waiting for transfers between devices: 0.01 us -> 135 us  [spread(): lax.all_to_all(jnp.stack([features] * lax.axis_size('nodes')), 'nodes', 0...]
    all_gather x2 -> x0, waiting for transfers between devices: 104 us -> none  [spread(): whole = lax.all_gather(features, 'nodes', axis=0, tiled=True)]
    all_to_all x1, waiting for transfers between devices: 151 us -> 171 us  [body(): lax.all_to_all(packed, 'nodes', split_axis=0, concat_axis=0, tiled=True)]
  transfers between devices with their start and end apart: 7 -> 5, of which waited for: 5 -> 4; matrix products, arithmetic and copies ran while one was open for 11% -> 7% of each run, Pallas kernels for 0% -> 0%
where the time goes in v1:
time: 859 us; the launch traced here: 858 us
  waiting for transfers between devices  497 us (58%)
  blocking collectives  242 us (28%)
  local copies, waits for them, and re-layouts  62.5 us (7%)
  matrix products  20.7 us (2%)
  starting transfers between devices  14.5 us (2%)
  between operations  13.9 us (2%)
    all_to_all x1, blocking collectives, spread(): lax.all_to_all(jnp.stack([features] * lax.axis_size('nodes')), 'nodes', 0...  191 us
    psum x1, waiting for transfers between devices, body(): grad_one, grad_two = lax.psum((grad_one, grad_two), 'nodes')  184 us
    all_to_all x1, waiting for transfers between devices, body(): lax.all_to_all(packed, 'nodes', split_axis=0, concat_axis=0, tiled=True)  171 us
    all_to_all x1, waiting for transfers between devices, spread(): lax.all_to_all(jnp.stack([features] * lax.axis_size('nodes')), 'nodes', 0...  135 us
    reshape x2, local copies, waits for them, and re-layouts, body(): terms.reshape(tile_total, block_size, width)[source]  21.9 us
    all_to_all x1, blocking collectives, body(): lax.all_to_all(requests, 'nodes', split_axis=0, concat_axis=0, tiled=True)  20.4 us
  transfers between devices with their start and end apart: 5, of which 4 were waited for; matrix products, arithmetic and copies ran while one was open for 7% of the time, Pallas kernels for 0%

profile of v1, /device:TPU:2, one launch (start us, length us, event | category | flops | bytes accessed | tf_op | source)
XLA Modules:
  0.0 857.7 jit_solution(5115311893587993138)
XLA Ops:
  10.9 20.4 %all_to_all.24 = s32[64,1,2]{2,1,0:T(1,128)S(1)} all-to-all(s32[64,1,2]{2,1,0:T(1,128)S(1)} %bitcast.76), channel_id=1, replica_groups=mesh['nodes'=64,'feat'=4] {'nodes'}, dimensions={0} | all-to-all | bytes 1024 | tf_op jit(solution)/shard_map/all_to_all | solution.py:34
  31.3 6.1 stack.4
  37.5 6.7 all-to-all-start
  45.1 14.0 %all_gather.6 = bf16[512,512]{1,0:T(8,128)(2,1)S(1)} all-gather(bf16[512,128]{1,0:T(8,128)(2,1)S(1)} %copy-done.3), channel_id=1, replica_groups=mesh['nodes'=64,'feat'=4] {'feat'}, dimensions={1}, use_global_device_ids=true | all-gather | bytes 655360 | tf_op jit(solution)/shard_map/all_gather | solution.py:59
  61.2 3.6 fusion.5
  64.8 6.6 copy.27
  71.4 7.1 gather_fusion.2
  78.5 15.3 %copy.28 = f32[64,2,128,128]{3,1,2,0:T(2,128)} copy(f32[64,2,128,128]{3,2,1,0:T(8,128)} %bitcast.65) | data formatting | bytes 16777216 | tf_op jit(solution)/shard_map/reshape | solution.py:70
  93.8 134.6 %all-to-all-done = bf16[64,512,128]{2,1,0:T(8,128)(2,1)} async-done(((bf16[64,512,128]{2,1,0:T(8,128)(2,1)}), bf16[64,512,128]{2,1,0:T(8,128)(2,1)}, u32[]{:S(2)}, u32[]{:S(2)}) %all-to-all-start) | async-done | bytes 8388640 | tf_op jit(solution)/shard_map/all_to_all | solution.py:39
  228.4 7.5 all-to-all-start.3
  236.0 6.2 gather_fusion
  242.2 2.9 fusion
  245.0 2.2 fusion.7
  248.8 171.3 %all-to-all-done.3 = f32[64,2,128,128]{3,1,2,0:T(2,128)} async-done(((f32[64,2,128,128]{3,1,2,0:T(2,128)}), f32[64,2,128,128]{3,1,2,0:T(2,128)}, u32[]{:S(2)}, u32[]{:S(2)}) %all-to-all-start.3) | async-done | bytes 8388640 | tf_op jit(solution)/shard_map/all_to_all | solution.py:73
  420.2 6.1 copy.29
  426.3 2.8 fusion.14
  430.9 2.0 stack.5
  432.9 191.3 %all_to_all.25 = bf16[64,512,128]{2,1,0:T(8,128)(2,1)} all-to-all(bf16[64,512,128]{2,1,0:T(8,128)(2,1)S(1)} %stack.5), channel_id=1, replica_groups=mesh['nodes'=64,'feat'=4] {'nodes'}, dimensions={0} | all-to-all | bytes 16777216 | tf_op jit(solution)/shard_map/all_to_all | solution.py:39
  624.2 6.2 gather_fusion.1
  630.4 2.9 fusion.1
  633.3 2.2 fusion.10
  635.6 16.4 %all_gather.7 = bf16[512,512]{1,0:T(8,128)(2,1)S(1)} all-gather(bf16[512,128]{1,0:T(8,128)(2,1)S(1)} %copy-done.2), channel_id=1, replica_groups=mesh['nodes'=64,'feat'=4] {'feat'}, dimensions={1}, use_global_device_ids=true | all-gather | bytes 655360 | tf_op jit(solution)/shard_map/all_gather | solution.py:83
  655.0 7.1 reduce-scatter.5.cloned.1.call-done
  663.7 184.2 %all-reduce.3.cloned.1.call-done = (f32[128,512]{1,0:T(8,128)}, f32[128,512]{1,0:T(8,128)}) async-done(((f32[128,512]{1,0:T(8,128)}, f32[128,512]{1,0:T(8,128)}), (f32[128,512]{1,0:T(8,128)}, f32[128,512]{1,0:T(8,128)})) %all-reduce.3.cloned.1.call-update) | async-done | bytes 524304 | tf_op jit(solution)/shard_map/psum | solution.py:88
  (38 shorter events, 18.1 us)
Async XLA Ops:
  7.2 54.0 %copy-start = (bf16[4,24,128,128]{3,2,1,0:T(8,128)(2,1)S(1)}, bf16[4,24,128,128]{3,2,1,0:T(8,128)(2,1)}, u32[]{:S(2)}) copy-start(bf16[4,24,128,128]{3,2,1,0:T(8,128)(2,1)} %param.10) | copy-start | bytes 9437188
  37.5 7.6 copy-start.3
  37.5 191.0 %all-to-all-start = ((bf16[64,512,128]{2,1,0:T(8,128)(2,1)}), bf16[64,512,128]{2,1,0:T(8,128)(2,1)}, u32[]{:S(2)}, u32[]{:S(2)}) async-start(bf16[64,512,128]{2,1,0:T(8,128)(2,1)} %stack.4), calls=%async_computation | async-start | bytes 16777216 | tf_op jit(solution)/shard_map/all_to_all | solution.py:39
  59.1 0.8 copy-start.1
  228.4 191.7 %all-to-all-start.3 = ((f32[64,2,128,128]{3,1,2,0:T(2,128)}), f32[64,2,128,128]{3,1,2,0:T(2,128)}, u32[]{:S(2)}, u32[]{:S(2)}) async-start(f32[64,2,128,128]{3,1,2,0:T(2,128)} %copy.28), calls=%async_computation.5 | async-start | bytes 16777216 | tf_op jit(solution)/shard_map/all_to_all | solution.py:73
  235.9 193.2 %reduce-scatter.3.cloned.1.call-start = ((), (), s32[]{:S(2)}) async-start(), calls=%async_computation.6 | async-start | bytes 1310720 | tf_op jit(solution)/shard_map/reduce_scatter | solution.py:49
  247.2 414.8 %reduce-scatter.5.cloned.1.call-start = ((), (), s32[]{:S(2)}) async-start(), calls=%async_computation.7 | async-start | bytes 1310720 | tf_op jit(solution)/shard_map/reduce_scatter | solution.py:49
  630.4 5.2 copy-start.2
  635.5 212.3 %all-reduce.3.cloned.1.call-start = ((), (), s32[]{:S(2)}) async-start(), calls=%async_computation.8 | async-start | bytes 1048576 | tf_op jit(solution)/shard_map/psum | solution.py:88
Sparse Core Ops, SparseCore 0:
  247.3 27.5 reduce-scatter.2
  635.6 26.3 reduce-scatter.4
  666.2 181.5 all-reduce.2
